TPU v7x, 32 devices: a whole 2x2x4 slice. The times are simulated.
32 devices in a mesh: groups: 2 (over y), ctx: 4 (over z), dp: 2 (over x), rep: 2 (over core).
Axes of the slice: x: 2, y: 2, z: 4, core: 2. Of those that a mesh axis runs over, the one named last changes fastest.
Arguments:
- features: float32 [8, 4096, 128], P(('groups', 'dp', 'rep'), 'ctx'), parts along dimension 0, may hold values from -6 to 6
- cotangent: float32 [8, 4096, 128], P(('groups', 'dp', 'rep'), 'ctx'), parts along dimension 0, may hold values from -6 to 6
- norm_gains: float32 [2, 128], replicated, may hold values from 0.5 to 1.5
- depth_taps: float32 [2, 7, 128], replicated, may hold values from -2 to 2
- w_in: float32 [2, 128, 256], replicated, may hold values from -0.5 to 0.5
- w_out: float32 [2, 256, 128], replicated, may hold values from -0.375 to 0.375
Outputs:
- grad_features: float32 [8, 4096, 128], P(('groups', 'dp', 'rep'), 'ctx'), parts along dimension 0
- grad_gains: float32 [4, 128], P('groups'), parts along dimension 0
- grad_taps: float32 [4, 7, 128], P('groups'), parts along dimension 0
- grad_w_in: float32 [4, 128, 256], P('groups'), parts along dimension 0
- grad_w_out: float32 [4, 256, 128], P('groups'), parts along dimension 0
There are 2 independent parts, one for each index of `groups`. A program takes and returns all parts, laid end to end along the dimension named above; an argument that names none is the same for every part. Nothing has to cross between parts.
All inputs are finite; a program needn't handle non-finite values.
Results may differ from a plain program's by a relative error of at most 0.0001.
Values sent between devices are 32-bit elements; how exact they have to be, the bound alone decides.
A program may use at most 64 MiB of HBM per device.

v0:
```python
import jax
import jax.numpy as jnp
from jax import lax
from jax.sharding import PartitionSpec as P

FIRST_SPACING = 16
SECOND_SPACING = 256
BLOCKS = 2
STABILIZER = 1e-06


def with_halo(block, sides, width):
    for axis, dim in sides:
        count = lax.axis_size(axis)
        forward = [(i, i + 1) for i in range(count - 1)]
        backward = [(target, source) for source, target in forward]
        low = lax.ppermute(
            lax.slice_in_dim(block, block.shape[dim] - width, None, axis=dim), axis, forward
        )
        high = lax.ppermute(lax.slice_in_dim(block, 0, width, axis=dim), axis, backward)
        block = jnp.concatenate([low, block, high], axis=dim)
    return block


def rms_norm(stream, gain_vec):
    scale = lax.rsqrt(jnp.mean(stream * stream, axis=-1, keepdims=True) + STABILIZER)
    return stream * scale * gain_vec


def depth_sweep(padded, tap_weights, dilation, row_count):
    total = tap_weights[0] * padded[:, 0:row_count]
    for offset in range(1, tap_weights.shape[0]):
        total = (
            total
            + tap_weights[offset] * padded[:, offset * dilation : offset * dilation + row_count]
        )
    return total


def forward_block(stream, gain_vec, tap_weights, w_in, w_out, dilation):
    rim_width = tap_weights.shape[0] // 2 * dilation
    normed = rms_norm(stream, gain_vec)
    padded = with_halo(normed, (("ctx", 1),), rim_width)
    conv_out = depth_sweep(padded, tap_weights, dilation, stream.shape[1])
    pre_act = jnp.einsum("brc,ch->brh", conv_out, w_in, precision=lax.Precision.HIGHEST)
    act_out = jax.nn.silu(pre_act)
    result = stream + jnp.einsum("brh,hc->brc", act_out, w_out, precision=lax.Precision.HIGHEST)
    return (result, (stream, padded, conv_out, pre_act, act_out))


def backward_block(grad_out, saved_state, gain_vec, tap_weights, w_in, w_out, dilation):
    stream, padded, conv_out, pre_act, act_out = saved_state
    row_count = stream.shape[1]
    tap_count = tap_weights.shape[0]
    rim_width = tap_count // 2 * dilation
    grad_wout = jnp.einsum("brh,brc->hc", act_out, grad_out, precision=lax.Precision.HIGHEST)
    activation_gradient = jnp.einsum(
        "brc,hc->brh", grad_out, w_out, precision=lax.Precision.HIGHEST
    )
    sigmoid_val = jax.nn.sigmoid(pre_act)
    grad_pre = activation_gradient * (sigmoid_val * (1.0 + pre_act * (1.0 - sigmoid_val)))
    grad_win = jnp.einsum("brc,brh->ch", conv_out, grad_pre, precision=lax.Precision.HIGHEST)
    grad_conv = jnp.einsum("brh,ch->brc", grad_pre, w_in, precision=lax.Precision.HIGHEST)
    grad_tapw = jnp.stack(
        [
            jnp.sum(
                grad_conv * padded[:, offset * dilation : offset * dilation + row_count],
                axis=(0, 1),
            )
            for offset in range(tap_count)
        ]
    )
    grad_rims = with_halo(grad_conv, (("ctx", 1),), rim_width)
    grad_norm = depth_sweep(grad_rims, tap_weights[::-1], dilation, row_count)
    unused_out, norm_back = jax.vjp(rms_norm, stream, gain_vec)
    grad_stream, grad_gain = norm_back(grad_norm)
    return (grad_stream + grad_out, (grad_gain, grad_tapw, grad_win, grad_wout))


def local(features, cotangent, norm_gains, depth_taps, w_in, w_out):
    spacing_list = (FIRST_SPACING, SECOND_SPACING)
    stream = features
    saved_list = []
    for block_index in range(BLOCKS):
        stream, saved_state = forward_block(
            stream,
            norm_gains[block_index],
            depth_taps[block_index],
            w_in[block_index],
            w_out[block_index],
            spacing_list[block_index],
        )
        saved_list.append(saved_state)
    grad_flow = cotangent
    block_grads = [None] * BLOCKS
    for block_index in reversed(range(BLOCKS)):
        grad_flow, local_grads = backward_block(
            grad_flow,
            saved_list[block_index],
            norm_gains[block_index],
            depth_taps[block_index],
            w_in[block_index],
            w_out[block_index],
            spacing_list[block_index],
        )
        block_grads[block_index] = local_grads
    gain_total = jnp.stack([block_grads[index_b][0] for index_b in range(BLOCKS)])
    taps_total = jnp.stack([block_grads[index_b][1] for index_b in range(BLOCKS)])
    input_weight_sum = jnp.stack([block_grads[index_b][2] for index_b in range(BLOCKS)])
    wout_total = jnp.stack([block_grads[index_b][3] for index_b in range(BLOCKS)])
    gain_total, taps_total, input_weight_sum, wout_total = lax.psum(
        (gain_total, taps_total, input_weight_sum, wout_total), ("ctx", "dp", "rep")
    )
    return (grad_flow, gain_total, taps_total, input_weight_sum, wout_total)


def solution(mesh):
    return jax.shard_map(
        local,
        mesh=mesh,
        in_specs=(
            P(("groups", "dp", "rep"), "ctx", None),
            P(("groups", "dp", "rep"), "ctx", None),
            P(),
            P(),
            P(),
            P(),
        ),
        out_specs=(
            P(("groups", "dp", "rep"), "ctx", None),
            P("groups", None),
            P("groups", None, None),
            P("groups", None, None),
            P("groups", None, None),
        ),
        check_vma=False,
    )
```

profile of v0, /device:TPU:1, one launch (start us, length us, event | category | flops | bytes accessed | tf_op | source)
XLA Modules:
  0.0 171.0 jit_solution(2257633979996218653)
XLA Ops:
  7.2 0.0 copy-start
  7.2 0.0 all-reduce.4.cloned.1.call-start
  7.2 0.8 slice_bitcast_fusion.5
  8.0 1.2 multiply_reduce_fusion.19
  9.3 0.2 multiply_multiply_fusion.1
  9.5 0.0 copy-start.20
  9.5 1.3 collective-permute-start.1
  10.8 4.7 %collective-permute-start = (f32[1,48,128]{2,1,0:T(8,128)S(1)}, f32[1,48,128]{2,1,0:T(8,128)S(1)}, u32[]{:S(2)}, u32[]{:S(2)}) collective-permute-start(f32[1,48,128]{2,1,0:T(8,128)S(1)} %get-tuple-element.47), channel_id=1, source_target_pairs={{0,4},{4,8},{8,12},{1,5},{5,9},{9,13},{2,6},{6,10},{10,14},{3,7},{... | collective-permute-start | bytes 73736 | tf_op jit(solution)/shard_map/ppermute | solution.py:17
  15.6 0.0 collective-permute-done.1
  15.7 0.0 copy-start.11
  15.7 0.7 collective-permute-done
  16.5 0.0 copy-start.9
  16.5 0.2 multiply_add_fusion.1
  16.7 0.3 copy-done.13
  17.0 0.4 copy-done.9
  17.4 1.0 fusion.51
  18.4 1.2 multiply_reduce_fusion.18
  19.6 0.2 multiply_multiply_fusion
  19.8 0.1 fusion.83
  19.9 1.3 collective-permute-start.3
  21.2 4.3 %collective-permute-start.2 = (f32[1,768,128]{2,1,0:T(8,128)S(1)}, f32[1,768,128]{2,1,0:T(8,128)S(1)}, u32[]{:S(2)}, u32[]{:S(2)}) collective-permute-start(f32[1,768,128]{2,1,0:T(8,128)S(1)} %get-tuple-element.45), channel_id=1, source_target_pairs={{0,4},{4,8},{8,12},{1,5},{5,9},{9,13},{2,6},{6,10},{10,14},{3,7},{... | collective-permute-start | bytes 1179656 | tf_op jit(solution)/shard_map/ppermute | solution.py:17
  25.5 5.6 %collective-permute-done.3 = f32[1,768,128]{2,1,0:T(8,128)S(1)} collective-permute-done((f32[1,768,128]{2,1,0:T(8,128)S(1)}, f32[1,768,128]{2,1,0:T(8,128)S(1)}, u32[]{:S(2)}, u32[]{:S(2)}) %collective-permute-start.3) | collective-permute-done | bytes 393248 | tf_op jit(solution)/shard_map/ppermute | solution.py:20
  31.1 0.9 collective-permute-done.2
  32.1 0.2 multiply_add_fusion
  32.3 0.0 copy-start.6
  32.3 1.0 fusion.48
  33.3 1.0 copy-done.3
  34.3 1.1 convolution_multiply_fusion.1
  35.4 1.7 multiply_reduce_fusion
  37.1 0.9 fusion.82
  38.1 4.1 %collective-permute-start.4 = (f32[1,768,128]{2,1,0:T(8,128)}, f32[1,768,128]{2,1,0:T(8,128)S(1)}, u32[]{:S(2)}, u32[]{:S(2)}) collective-permute-start(f32[1,768,128]{2,1,0:T(8,128)} %get-tuple-element.42), channel_id=1, source_target_pairs={{0,4},{4,8},{8,12},{1,5},{5,9},{9,13},{2,6},{6,10},{10,14},{3,7},{... | collective-permute-start | bytes 1179656 | tf_op jit(solution)/shard_map/ppermute | solution.py:17
  42.2 1.5 collective-permute-start.5
  43.7 1.3 stack.103
  45.0 2.4 %convolution_bitcast_fusion.3 = f32[1,128,256]{2,1,0:T(8,128)S(1)} fusion(f32[1024,256]{1,0:T(8,128)} %copy-done.5, f32[1,1024,128]{2,1,0:T(8,128)S(1)} %multiply_add_fusion), kind=kOutput, calls=%fused_computation.6 | convolution fusion | flops 402653184 | bytes 1703936 | tf_op jit(solution)/shard_map/brc,brh->ch/dot_general | solution.py:62
  47.4 0.0 copy-start.19
  47.4 1.9 %convolution_bitcast_fusion.1 = f32[1,256,128]{2,1,0:T(8,128)S(1)} fusion(f32[1024,256]{1,0:T(8,128)S(1)} %copy-done.4, f32[1,1024,128]{2,1,0:T(8,128)S(1)} %copy-done.7), kind=kOutput, calls=%fused_computation.4 | convolution fusion | flops 403701760 | bytes 1703936 | tf_op jit(solution)/shard_map/brh,brc->hc/dot_general | solution.py:56
  49.3 0.0 collective-permute-done.4
  49.4 2.6 %collective-permute-done.5 = f32[1,768,128]{2,1,0:T(8,128)} collective-permute-done((f32[1,768,128]{2,1,0:T(8,128)}, f32[1,768,128]{2,1,0:T(8,128)}, u32[]{:S(2)}, u32[]{:S(2)}) %collective-permute-start.5) | collective-permute-done | bytes 393248 | tf_op jit(solution)/shard_map/ppermute | solution.py:20
  52.0 1.7 multiply_reduce_fusion.14
  53.7 0.3 fusion.21
  54.1 0.9 copy-done.2
  54.9 1.9 %convolution_bitcast_fusion.2 = f32[1,256,128]{2,1,0:T(8,128)S(1)} fusion(f32[1,1024,128]{2,1,0:T(8,128)S(1)} %fusion.21, f32[1024,256]{1,0:T(8,128)S(1)} %copy-done.2), kind=kOutput, calls=%fused_computation.5 | convolution fusion | flops 403701760 | bytes 1703936 | tf_op jit(solution)/shard_map/brh,brc->hc/dot_general | solution.py:56
  56.8 1.1 convolution_multiply_fusion
  58.0 0.0 copy-start.10
  58.0 0.0 copy-start.12
  58.0 0.0 copy-start.14
  58.0 1.0 convolution_bitcast_fusion.4
  59.1 1.0 multiply_reduce_fusion.7
  60.1 2.8 %collective-permute-start.6 = (f32[1,48,128]{2,1,0:T(8,128)S(1)}, f32[1,48,128]{2,1,0:T(8,128)S(1)}, u32[]{:S(2)}, u32[]{:S(2)}) collective-permute-start(f32[1,48,128]{2,1,0:T(8,128)S(1)} %get-tuple-element.40), channel_id=1, source_target_pairs={{0,4},{4,8},{8,12},{1,5},{5,9},{9,13},{2,6},{6,10},{10,14},{3,7},{... | collective-permute-start | bytes 73736 | tf_op jit(solution)/shard_map/ppermute | solution.py:17
  62.9 1.3 collective-permute-start.7
  64.2 0.7 pad_maximum_fusion.8
  65.0 0.7 pad_maximum_fusion.9
  65.7 0.0 all-reduce.4.cloned.1.call-update
  65.7 0.0 copy-start.15
  65.7 0.7 copy-done.15
  66.5 0.0 collective-permute-done.6
  66.5 1.0 collective-permute-done.7
  67.6 0.5 multiply_reduce_fusion.15
  68.1 36.3 %all-reduce = (f32[2,128]{1,0:T(2,128)}, f32[2,7,128]{2,1,0:T(8,128)S(1)}) all-reduce(f32[2,128]{1,0:T(2,128)S(1)} %pad_maximum_fusion.11, f32[2,7,128]{2,1,0:T(8,128)S(1)} %pad_maximum_fusion.10), channel_id=1, replica_groups=mesh['groups'=2,'ctx'=4,'dp'=2,'rep'=2] {'ctx','dp','rep'}, use_global_device_ids=true, to_apply=%region_6.7 | all-reduce | flops 2048 | bytes 16384 | tf_op jit(solution)/shard_map/psum | solution.py:111
  104.4 0.6 copy.11
  105.0 1.1 fusion.22
  106.1 55.6 %all-reduce.4.cloned.1.call-done = (f32[2,128,256]{2,1,0:T(8,128)}, f32[2,256,128]{2,1,0:T(8,128)}) async-done(((f32[2,128,256]{2,1,0:T(8,128)}, f32[2,256,128]{2,1,0:T(8,128)}), (f32[2,128,256]{2,1,0:T(8,128)}, f32[2,256,128]{2,1,0:T(8,128)})) %all-reduce.4.cloned.1.call-update) | async-done | bytes 524304 | tf_op jit(solution)/shard_map/psum | solution.py:111
  161.7 1.7 %copy.14 = f32[2,128,256]{2,1,0:T(8,128)} copy(f32[2,128,256]{2,1,0:T(8,128)} %get-tuple-element.71) | data formatting | bytes 524288
  163.4 0.7 copy.15
  (97 shorter events, 0.3 us)
Async XLA Ops:
  7.2 2.1 %copy-start = (f32[1,1024,128]{2,1,0:T(8,128)S(1)}, f32[1,1024,128]{2,1,0:T(8,128)}, u32[]{:S(2)}) copy-start(f32[1,1024,128]{2,1,0:T(8,128)} %param.6) | copy-start | bytes 1572868
  7.2 154.5 %all-reduce.4.cloned.1.call-start = ((), (), s32[]{:S(2)}) async-start(), calls=%async_computation | async-start | bytes 1048576 | tf_op jit(solution)/shard_map/psum | solution.py:111
  8.0 1.3 copy-start.16
  8.0 11.6 %copy-start.18 = (f32[128]{0:T(128)}, f32[128]{0:T(128)S(1)}, u32[]{:S(2)}) copy-start(f32[128]{0:T(128)S(1)} %get-tuple-element.62) | copy-start | bytes 1540
  9.5 6.0 %copy-start.20 = (f32[2,7,128]{2,0,1:T(2,128)S(1)}, f32[2,7,128]{2,0,1:T(2,128)}, u32[]{:S(2)}) copy-start(f32[2,7,128]{2,0,1:T(2,128)} %param.9) | copy-start | bytes 21508
  9.5 6.1 %collective-permute-start.1 = (f32[1,48,128]{2,1,0:T(8,128)S(1)}, f32[1,48,128]{2,1,0:T(8,128)S(1)}, u32[]{:S(2)}, u32[]{:S(2)}) collective-permute-start(f32[1,48,128]{2,1,0:T(8,128)S(1)} %get-tuple-element.46), channel_id=1, source_target_pairs={{4,0},{8,4},{12,8},{5,1},{9,5},{13,9},{6,2},{10,6},{14,10},{7,3},{... | collective-permute-start | bytes 73736 | tf_op jit(solution)/shard_map/ppermute | solution.py:20
  10.8 5.6 %collective-permute-start = (f32[1,48,128]{2,1,0:T(8,128)S(1)}, f32[1,48,128]{2,1,0:T(8,128)S(1)}, u32[]{:S(2)}, u32[]{:S(2)}) collective-permute-start(f32[1,48,128]{2,1,0:T(8,128)S(1)} %get-tuple-element.47), channel_id=1, source_target_pairs={{0,4},{4,8},{8,12},{1,5},{5,9},{9,13},{2,6},{6,10},{10,14},{3,7},{... | collective-permute-start | bytes 73736 | tf_op jit(solution)/shard_map/ppermute | solution.py:17
  15.5 0.9 copy-start.21
  15.5 0.9 copy-start.23
  15.5 0.9 copy-start.25
  15.5 0.9 copy-start.27
  15.5 0.9 copy-start.29
  15.6 0.9 copy-start.31
  15.6 0.9 copy-start.33
  15.6 16.4 %copy-start.35 = (f32[128]{0:T(128)}, f32[128]{0:T(128)S(1)}, u32[]{:S(2)}) copy-start(f32[128]{0:T(128)S(1)} %get-tuple-element.48) | copy-start | bytes 1540
  15.6 16.4 %copy-start.37 = (f32[128]{0:T(128)}, f32[128]{0:T(128)S(1)}, u32[]{:S(2)}) copy-start(f32[128]{0:T(128)S(1)} %get-tuple-element.49) | copy-start | bytes 1540
  15.6 16.4 %copy-start.39 = (f32[128]{0:T(128)}, f32[128]{0:T(128)S(1)}, u32[]{:S(2)}) copy-start(f32[128]{0:T(128)S(1)} %get-tuple-element.50) | copy-start | bytes 1540
  15.6 16.4 %copy-start.41 = (f32[128]{0:T(128)}, f32[128]{0:T(128)S(1)}, u32[]{:S(2)}) copy-start(f32[128]{0:T(128)S(1)} %get-tuple-element.51) | copy-start | bytes 1540
  15.6 16.4 %copy-start.43 = (f32[128]{0:T(128)}, f32[128]{0:T(128)S(1)}, u32[]{:S(2)}) copy-start(f32[128]{0:T(128)S(1)} %get-tuple-element.58) | copy-start | bytes 1540
  15.6 16.4 %copy-start.45 = (f32[128]{0:T(128)}, f32[128]{0:T(128)S(1)}, u32[]{:S(2)}) copy-start(f32[128]{0:T(128)S(1)} %get-tuple-element.60) | copy-start | bytes 1540
  15.6 16.4 %copy-start.47 = (f32[128]{0:T(128)}, f32[128]{0:T(128)S(1)}, u32[]{:S(2)}) copy-start(f32[128]{0:T(128)S(1)} %get-tuple-element.61) | copy-start | bytes 1540
  15.7 1.1 copy-start.11
  16.4 0.6 copy-start.13
  16.5 1.0 copy-start.9
  17.4 1.0 copy-start.49
  18.4 1.2 copy-start.1
  19.9 11.2 %collective-permute-start.3 = (f32[1,768,128]{2,1,0:T(8,128)S(1)}, f32[1,768,128]{2,1,0:T(8,128)S(1)}, u32[]{:S(2)}, u32[]{:S(2)}) collective-permute-start(f32[1,768,128]{2,1,0:T(8,128)S(1)} %get-tuple-element.44), channel_id=1, source_target_pairs={{4,0},{8,4},{12,8},{5,1},{9,5},{13,9},{6,2},{10,6},{14,10},{7,3},{... | collective-permute-start | bytes 1179656 | tf_op jit(solution)/shard_map/ppermute | solution.py:20
  21.2 10.8 %collective-permute-start.2 = (f32[1,768,128]{2,1,0:T(8,128)S(1)}, f32[1,768,128]{2,1,0:T(8,128)S(1)}, u32[]{:S(2)}, u32[]{:S(2)}) collective-permute-start(f32[1,768,128]{2,1,0:T(8,128)S(1)} %get-tuple-element.45), channel_id=1, source_target_pairs={{0,4},{4,8},{8,12},{1,5},{5,9},{9,13},{2,6},{6,10},{10,14},{3,7},{... | collective-permute-start | bytes 1179656 | tf_op jit(solution)/shard_map/ppermute | solution.py:17
  32.3 2.0 %copy-start.6 = (f32[1,1024,128]{2,1,0:T(8,128)S(1)}, f32[1,1024,128]{2,1,0:T(8,128)}, u32[]{:S(2)}) copy-start(f32[1,1024,128]{2,1,0:T(8,128)} %param.7) | copy-start | bytes 1572868
  33.3 1.0 copy-start.3
  35.4 1.7 %copy-start.5 = (f32[1024,256]{1,0:T(8,128)}, f32[1024,256]{1,0:T(8,128)S(1)}, u32[]{:S(2)}) copy-start(f32[1024,256]{1,0:T(8,128)S(1)} %convolution_multiply_fusion.1) | copy-start | bytes 3145732
  38.1 11.3 %collective-permute-start.4 = (f32[1,768,128]{2,1,0:T(8,128)}, f32[1,768,128]{2,1,0:T(8,128)S(1)}, u32[]{:S(2)}, u32[]{:S(2)}) collective-permute-start(f32[1,768,128]{2,1,0:T(8,128)} %get-tuple-element.42), channel_id=1, source_target_pairs={{0,4},{4,8},{8,12},{1,5},{5,9},{9,13},{2,6},{6,10},{10,14},{3,7},{... | collective-permute-start | bytes 1179656 | tf_op jit(solution)/shard_map/ppermute | solution.py:17
  42.2 9.8 %collective-permute-start.5 = (f32[1,768,128]{2,1,0:T(8,128)}, f32[1,768,128]{2,1,0:T(8,128)}, u32[]{:S(2)}, u32[]{:S(2)}) collective-permute-start(f32[1,768,128]{2,1,0:T(8,128)} %get-tuple-element.43), channel_id=1, source_target_pairs={{4,0},{8,4},{12,8},{5,1},{9,5},{13,9},{6,2},{10,6},{14,10},{7,3},{... | collective-permute-start | bytes 1179656 | tf_op jit(solution)/shard_map/ppermute | solution.py:20
  45.0 2.4 %copy-start.4 = (f32[1024,256]{1,0:T(8,128)S(1)}, f32[1024,256]{1,0:T(8,128)}, u32[]{:S(2)}) copy-start(f32[1024,256]{1,0:T(8,128)} %copy-done.3) | copy-start | bytes 3145732
  45.0 2.4 %copy-start.7 = (f32[1,1024,128]{2,1,0:T(8,128)S(1)}, f32[1,1024,128]{2,1,0:T(8,128)}, u32[]{:S(2)}) copy-start(f32[1,1024,128]{2,1,0:T(8,128)} %param.7) | copy-start | bytes 1572868
  47.4 4.6 %copy-start.19 = (f32[128]{0:T(128)S(1)}, f32[128]{0:T(128)}, u32[]{:S(2)}) copy-start(f32[128]{0:T(128)} %copy-done.18) | copy-start | bytes 1540
  47.4 4.6 %copy-start.36 = (f32[128]{0:T(128)S(1)}, f32[128]{0:T(128)}, u32[]{:S(2)}) copy-start(f32[128]{0:T(128)} %copy-done.35) | copy-start | bytes 1540
  47.4 4.6 %copy-start.38 = (f32[128]{0:T(128)S(1)}, f32[128]{0:T(128)}, u32[]{:S(2)}) copy-start(f32[128]{0:T(128)} %copy-done.37) | copy-start | bytes 1540
  47.4 4.6 %copy-start.40 = (f32[128]{0:T(128)S(1)}, f32[128]{0:T(128)}, u32[]{:S(2)}) copy-start(f32[128]{0:T(128)} %copy-done.39) | copy-start | bytes 1540
  47.4 4.6 %copy-start.42 = (f32[128]{0:T(128)S(1)}, f32[128]{0:T(128)}, u32[]{:S(2)}) copy-start(f32[128]{0:T(128)} %copy-done.41) | copy-start | bytes 1540
  47.4 4.6 %copy-start.44 = (f32[128]{0:T(128)S(1)}, f32[128]{0:T(128)}, u32[]{:S(2)}) copy-start(f32[128]{0:T(128)} %copy-done.43) | copy-start | bytes 1540
  47.4 4.6 %copy-start.46 = (f32[128]{0:T(128)S(1)}, f32[128]{0:T(128)}, u32[]{:S(2)}) copy-start(f32[128]{0:T(128)} %copy-done.45) | copy-start | bytes 1540
  47.4 4.6 %copy-start.48 = (f32[128]{0:T(128)S(1)}, f32[128]{0:T(128)}, u32[]{:S(2)}) copy-start(f32[128]{0:T(128)} %copy-done.47) | copy-start | bytes 1540
  53.7 1.2 copy-start.2
  54.9 1.9 %copy-start.50 = (f32[2,256,128]{2,1,0:T(8,128)S(1)}, f32[2,256,128]{2,1,0:T(8,128)}, u32[]{:S(2)}) copy-start(f32[2,256,128]{2,1,0:T(8,128)} %param.11) | copy-start | bytes 786436
  58.0 1.1 copy-start.10
  58.0 1.1 copy-start.12
  58.0 1.1 copy-start.14
  60.1 6.3 %collective-permute-start.6 = (f32[1,48,128]{2,1,0:T(8,128)S(1)}, f32[1,48,128]{2,1,0:T(8,128)S(1)}, u32[]{:S(2)}, u32[]{:S(2)}) collective-permute-start(f32[1,48,128]{2,1,0:T(8,128)S(1)} %get-tuple-element.40), channel_id=1, source_target_pairs={{0,4},{4,8},{8,12},{1,5},{5,9},{9,13},{2,6},{6,10},{10,14},{3,7},{... | collective-permute-start | bytes 73736 | tf_op jit(solution)/shard_map/ppermute | solution.py:17
  62.9 4.6 %collective-permute-start.7 = (f32[1,48,128]{2,1,0:T(8,128)S(1)}, f32[1,48,128]{2,1,0:T(8,128)S(1)}, u32[]{:S(2)}, u32[]{:S(2)}) collective-permute-start(f32[1,48,128]{2,1,0:T(8,128)S(1)} %get-tuple-element.41), channel_id=1, source_target_pairs={{4,0},{8,4},{12,8},{5,1},{9,5},{13,9},{6,2},{10,6},{14,10},{7,3},{... | collective-permute-start | bytes 73736 | tf_op jit(solution)/shard_map/ppermute | solution.py:20
  65.7 0.7 copy-start.15
  66.4 1.1 copy-start.17
  66.4 1.1 copy-start.22
  66.4 1.1 copy-start.24
  66.4 1.1 copy-start.26
  66.4 1.1 copy-start.28
  66.4 1.1 copy-start.30
  66.4 1.1 copy-start.32
  66.4 1.1 copy-start.34
  161.7 1.7 %copy-start.8 = (f32[2,256,128]{2,1,0:T(8,128)S(1)}, f32[2,256,128]{2,1,0:T(8,128)}, u32[]{:S(2)}) copy-start(f32[2,256,128]{2,1,0:T(8,128)} %get-tuple-element.72) | copy-start | bytes 786436
Sparse Core Ops, SparseCore 0:
  65.8 95.8 all-reduce.3
where the time goes:
time: 172 us; the launch traced here: 171 us
  waiting for transfers between devices  66.6 us (39%)
  blocking collectives  36.3 us (21%)
  starting transfers between devices  21.3 us (12%)
  matrix products  15.3 us (9%)
  between operations  14.9 us (9%)
  local copies, waits for them, and re-layouts  9.53 us (6%)
  other arithmetic  7.23 us (4%)
    psum x1, waiting for transfers between devices, local(): lax.psum((gain_total, taps_total, input_weight_sum, wout_total), ('ctx',...  55.6 us
    psum x1, blocking collectives, local(): lax.psum((gain_total, taps_total, input_weight_sum, wout_total), ('ctx',...  36.3 us
    ppermute x4, starting transfers between devices, with_halo(): lax.ppermute(lax.slice_in_dim(block, block.shape[dim] - width, None, axis...  15.9 us
    ppermute x4, waiting for transfers between devices, with_halo(): lax.ppermute(lax.slice_in_dim(block, 0, width, axis=dim), axis, backward)  9.29 us
    unnamed x105, local copies, waits for them, and re-layouts  6.46 us
    ppermute x4, starting transfers between devices, with_halo(): lax.ppermute(lax.slice_in_dim(block, 0, width, axis=dim), axis, backward)  5.35 us
    dot_general x2, matrix products, backward_block(): jnp.einsum('brh,brc->hc', act_out, grad_out, precision=lax.Precision.HIGH...  3.78 us
  transfers between devices with their start and end apart: 9, of which 6 were waited for; matrix products, arithmetic and copies ran while one was open for 5% of the time, Pallas kernels for 0%

commit v1 on v0

--- a/solution.py
+++ b/solution.py
@@ -1,12 +1,23 @@
+import functools
 import jax
 import jax.numpy as jnp
 from jax import lax
 from jax.sharding import PartitionSpec as P
+from jax.lax import psum
 
 FIRST_SPACING = 16
 SECOND_SPACING = 256
 BLOCKS = 2
 STABILIZER = 1e-06
+
+
+def space_start(inp, axis_tag, named_axis):
+    for dev_j in (axis_tag, named_axis):
+        inp = psum(inp, axis_name=dev_j)
+    return inp
+
+
+balance_the_shapes = functools.partial(space_start, axis_tag=("dp", "rep"), named_axis="ctx")
 
 
 def with_halo(block, sides, width):
@@ -108,8 +119,8 @@
     taps_total = jnp.stack([block_grads[index_b][1] for index_b in range(BLOCKS)])
     input_weight_sum = jnp.stack([block_grads[index_b][2] for index_b in range(BLOCKS)])
     wout_total = jnp.stack([block_grads[index_b][3] for index_b in range(BLOCKS)])
-    gain_total, taps_total, input_weight_sum, wout_total = lax.psum(
-        (gain_total, taps_total, input_weight_sum, wout_total), ("ctx", "dp", "rep")
+    gain_total, taps_total, input_weight_sum, wout_total = balance_the_shapes(
+        (gain_total, taps_total, input_weight_sum, wout_total)
     )
     return (grad_flow, gain_total, taps_total, input_weight_sum, wout_total)
 

time: 172 us -> 156 us (0.907)
  blocking collectives: 36.3 us -> 18.3 us
    psum x1 -> x2, blocking collectives: 36.3 us -> 18.3 us  [space_start(): inp = psum(inp, axis_name=dev_j)]
    psum x1 -> x2, waiting for transfers between devices: 55.6 us -> 56.4 us  [space_start(): inp = psum(inp, axis_name=dev_j)]
  transfers between devices with their start and end apart: 9 -> 10, of which waited for: 6 -> 7; matrix products, arithmetic and copies ran while one was open for 5% -> 6% of each run, Pallas kernels for 0% -> 0%
where the time goes in v1:
time: 156 us; the launch traced here: 154 us
  waiting for transfers between devices  67.3 us (43%)
  starting transfers between devices  21.3 us (14%)
  blocking collectives  18.3 us (12%)
  matrix products  15.3 us (10%)
  between operations  14.9 us (10%)
  local copies, waits for them, and re-layouts  9.53 us (6%)
  other arithmetic  7.23 us (5%)
    psum x2, waiting for transfers between devices, space_start(): inp = psum(inp, axis_name=dev_j)  56.4 us
    psum x2, blocking collectives, space_start(): inp = psum(inp, axis_name=dev_j)  18.3 us
    ppermute x4, starting transfers between devices, with_halo(): lax.ppermute(lax.slice_in_dim(block, block.shape[dim] - width, None, axis...  15.9 us
    ppermute x4, waiting for transfers between devices, with_halo(): lax.ppermute(lax.slice_in_dim(block, 0, width, axis=dim), axis, backward)  9.24 us
    unnamed x105, local copies, waits for them, and re-layouts  6.46 us
    ppermute x4, starting transfers between devices, with_halo(): lax.ppermute(lax.slice_in_dim(block, 0, width, axis=dim), axis, backward)  5.35 us
    dot_general x2, matrix products, backward_block(): jnp.einsum('brh,brc->hc', act_out, grad_out, precision=lax.Precision.HIGH...  3.78 us
    dot_general x2, matrix products, backward_block(): jnp.einsum('brc,brh->ch', conv_out, grad_pre, precision=lax.Precision.HIG...  3.41 us
  transfers between devices with their start and end apart: 10, of which 7 were waited for; matrix products, arithmetic and copies ran while one was open for 6% of the time, Pallas kernels for 0%

profile of v1, /device:TPU:1, one launch (start us, length us, event | category | flops | bytes accessed | tf_op | source)
XLA Modules:
  0.0 153.8 jit_solution(11035074428236820447)
XLA Ops:
  7.2 0.0 copy-start
  7.2 0.0 all-reduce.7.cloned.1.call-start
  7.2 0.8 slice_bitcast_fusion.5
  8.0 1.2 multiply_reduce_fusion.19
  9.3 0.2 multiply_multiply_fusion.1
  9.5 0.0 copy-start.20
  9.5 1.3 collective-permute-start.1
  10.8 4.7 %collective-permute-start = (f32[1,48,128]{2,1,0:T(8,128)S(1)}, f32[1,48,128]{2,1,0:T(8,128)S(1)}, u32[]{:S(2)}, u32[]{:S(2)}) collective-permute-start(f32[1,48,128]{2,1,0:T(8,128)S(1)} %get-tuple-element.51), channel_id=1, source_target_pairs={{0,4},{4,8},{8,12},{1,5},{5,9},{9,13},{2,6},{6,10},{10,14},{3,7},{... | collective-permute-start | bytes 73736 | tf_op jit(solution)/shard_map/ppermute | solution.py:28
  15.7 0.0 copy-start.11
  15.7 0.7 collective-permute-done
  16.5 0.0 copy-start.9
  16.5 0.2 multiply_add_fusion.1
  16.7 0.3 copy-done.13
  17.0 0.4 copy-done.9
  17.4 1.0 fusion.51
  18.4 1.2 multiply_reduce_fusion.18
  19.6 0.2 multiply_multiply_fusion
  19.8 0.1 fusion.83
  19.9 1.3 collective-permute-start.3
  21.2 4.3 %collective-permute-start.2 = (f32[1,768,128]{2,1,0:T(8,128)S(1)}, f32[1,768,128]{2,1,0:T(8,128)S(1)}, u32[]{:S(2)}, u32[]{:S(2)}) collective-permute-start(f32[1,768,128]{2,1,0:T(8,128)S(1)} %get-tuple-element.49), channel_id=1, source_target_pairs={{0,4},{4,8},{8,12},{1,5},{5,9},{9,13},{2,6},{6,10},{10,14},{3,7},{... | collective-permute-start | bytes 1179656 | tf_op jit(solution)/shard_map/ppermute | solution.py:28
  25.5 5.6 %collective-permute-done.3 = f32[1,768,128]{2,1,0:T(8,128)S(1)} collective-permute-done((f32[1,768,128]{2,1,0:T(8,128)S(1)}, f32[1,768,128]{2,1,0:T(8,128)S(1)}, u32[]{:S(2)}, u32[]{:S(2)}) %collective-permute-start.3) | collective-permute-done | bytes 393248 | tf_op jit(solution)/shard_map/ppermute | solution.py:31
  31.1 0.9 collective-permute-done.2
  32.1 0.2 multiply_add_fusion
  32.3 0.0 copy-start.6
  32.3 1.0 fusion.48
  33.3 1.0 copy-done.3
  34.3 1.1 convolution_multiply_fusion.1
  35.4 1.7 %multiply_reduce_fusion = (f32[128]{0:T(128)}, f32[128]{0:T(128)}, f32[128]{0:T(128)}, f32[128]{0:T(128)}, f32[128]{0:T(128)}, /*index=5*/f32[128]{0:T(128)}, f32[128]{0:T(128)}, f32[1024,128]{1,0:T(8,128)S(1)}) fusion(f32[1,768,128]{2,1,0:T(8,128)S(1)} %collective-permute-done.3, f32[1,1024,128]{2,1,0:T(8,128)S(1)} %multiply_multiply_fusion, ...), kind=kOutput, calls=%fused_computation.106 | convolution fusion | flops 405273728 | bytes 3018240 | tf_op jit(solution)/shard_map/brh,ch->brc/dot_general | solution.py:74
  37.1 0.9 fusion.82
  38.1 4.1 %collective-permute-start.4 = (f32[1,768,128]{2,1,0:T(8,128)}, f32[1,768,128]{2,1,0:T(8,128)S(1)}, u32[]{:S(2)}, u32[]{:S(2)}) collective-permute-start(f32[1,768,128]{2,1,0:T(8,128)} %get-tuple-element.46), channel_id=1, source_target_pairs={{0,4},{4,8},{8,12},{1,5},{5,9},{9,13},{2,6},{6,10},{10,14},{3,7},{... | collective-permute-start | bytes 1179656 | tf_op jit(solution)/shard_map/ppermute | solution.py:28
  42.2 1.5 collective-permute-start.5
  43.7 1.3 stack.103
  45.0 2.4 %convolution_bitcast_fusion.3 = f32[1,128,256]{2,1,0:T(8,128)S(1)} fusion(f32[1024,256]{1,0:T(8,128)} %copy-done.5, f32[1,1024,128]{2,1,0:T(8,128)S(1)} %multiply_add_fusion), kind=kOutput, calls=%fused_computation.6 | convolution fusion | flops 402653184 | bytes 1703936 | tf_op jit(solution)/shard_map/brc,brh->ch/dot_general | solution.py:73
  47.4 0.0 copy-start.19
  47.5 1.9 %convolution_bitcast_fusion.1 = f32[1,256,128]{2,1,0:T(8,128)S(1)} fusion(f32[1024,256]{1,0:T(8,128)S(1)} %copy-done.4, f32[1,1024,128]{2,1,0:T(8,128)S(1)} %copy-done.7), kind=kOutput, calls=%fused_computation.4 | convolution fusion | flops 403701760 | bytes 1703936 | tf_op jit(solution)/shard_map/brh,brc->hc/dot_general | solution.py:67
  49.4 2.6 %collective-permute-done.5 = f32[1,768,128]{2,1,0:T(8,128)} collective-permute-done((f32[1,768,128]{2,1,0:T(8,128)}, f32[1,768,128]{2,1,0:T(8,128)}, u32[]{:S(2)}, u32[]{:S(2)}) %collective-permute-start.5) | collective-permute-done | bytes 393248 | tf_op jit(solution)/shard_map/ppermute | solution.py:31
  52.0 1.7 %multiply_reduce_fusion.14 = (f32[128]{0:T(128)S(1)}, f32[1024]{0:T(1024)S(1)}, f32[1,1024,128]{2,1,0:T(8,128)S(1)}) fusion(f32[1,1024,128]{2,1,0:T(8,128)S(1)} %get-tuple-element.69, f32[1024]{0:T(1024)S(1)} %fusion.75, f32[128]{0:T(128)S(1)} %copy-done.19, f32[1,768,128]{2,1,0:T(8,128)} %collective-permute-done.5, f32[1,1024,128]{2,1,0:T(8,128)S(1)} %bitcast.133, ...), kind=kLoop, calls=%fused_computation.120 | loop fusion | flops 3275648 | bytes 2896384 | tf_op jit(solution)/shard_map/transpose(jvp())/reduce_sum | solution.py:38
  53.7 0.3 fusion.21
  54.1 0.9 copy-done.2
  54.9 1.9 %convolution_bitcast_fusion.2 = f32[1,256,128]{2,1,0:T(8,128)S(1)} fusion(f32[1,1024,128]{2,1,0:T(8,128)S(1)} %fusion.21, f32[1024,256]{1,0:T(8,128)S(1)} %copy-done.2), kind=kOutput, calls=%fused_computation.5 | convolution fusion | flops 403701760 | bytes 1703936 | tf_op jit(solution)/shard_map/brh,brc->hc/dot_general | solution.py:67
  56.8 1.1 convolution_multiply_fusion
  58.0 0.0 copy-start.10
  58.0 0.0 copy-start.12
  58.0 0.0 copy-start.14
  58.0 1.0 convolution_bitcast_fusion.4
  59.1 1.0 multiply_reduce_fusion.7
  60.1 2.8 %collective-permute-start.6 = (f32[1,48,128]{2,1,0:T(8,128)S(1)}, f32[1,48,128]{2,1,0:T(8,128)S(1)}, u32[]{:S(2)}, u32[]{:S(2)}) collective-permute-start(f32[1,48,128]{2,1,0:T(8,128)S(1)} %get-tuple-element.44), channel_id=1, source_target_pairs={{0,4},{4,8},{8,12},{1,5},{5,9},{9,13},{2,6},{6,10},{10,14},{3,7},{... | collective-permute-start | bytes 73736 | tf_op jit(solution)/shard_map/ppermute | solution.py:28
  62.9 1.3 collective-permute-start.7
  64.2 0.7 pad_maximum_fusion.8
  65.0 0.7 pad_maximum_fusion.9
  65.7 0.0 all-reduce.7.cloned.1.call-update
  65.7 0.0 all-reduce.9.cloned.1.call-start
  65.8 0.7 copy-done.15
  66.5 1.0 collective-permute-done.7
  67.6 0.5 multiply_reduce_fusion.15
  68.1 34.8 %all-reduce.7.cloned.1.call-done = (f32[2,128,256]{2,1,0:T(8,128)}, f32[2,256,128]{2,1,0:T(8,128)}) async-done(((f32[2,128,256]{2,1,0:T(8,128)}, f32[2,256,128]{2,1,0:T(8,128)}), (f32[2,128,256]{2,1,0:T(8,128)}, f32[2,256,128]{2,1,0:T(8,128)})) %all-reduce.7.cloned.1.call-update) | async-done | bytes 524304 | tf_op jit(solution)/shard_map/psum | solution.py:16
  102.8 0.0 all-reduce.9.cloned.1.call-update
  102.9 7.1 %all-reduce = (f32[2,128]{1,0:T(2,128)S(1)}, f32[2,7,128]{2,1,0:T(8,128)S(1)}) all-reduce(f32[2,128]{1,0:T(2,128)S(1)} %pad_maximum_fusion.11, f32[2,7,128]{2,1,0:T(8,128)S(1)} %pad_maximum_fusion.10), channel_id=1, replica_groups=mesh['groups'=2,'ctx'=4,'dp'=2,'rep'=2] {'dp','rep'}, use_global_device_ids=true, to_apply=%region_6.7 | all-reduce | flops 2048 | bytes 16384 | tf_op jit(solution)/shard_map/psum | solution.py:16
  110.0 11.1 %all-reduce.2 = (f32[2,128]{1,0:T(2,128)}, f32[2,7,128]{2,1,0:T(8,128)S(1)}) all-reduce(f32[2,128]{1,0:T(2,128)S(1)} %get-tuple-element.34, f32[2,7,128]{2,1,0:T(8,128)S(1)} %get-tuple-element.35), channel_id=1, replica_groups=mesh['groups'=2,'ctx'=4,'dp'=2,'rep'=2] {'ctx'}, use_global_device_ids=true, to_apply=%region_7.8 | all-reduce | flops 2048 | bytes 16384 | tf_op jit(solution)/shard_map/psum | solution.py:16
  121.1 0.6 copy.11
  121.7 1.1 fusion.22
  122.9 21.7 %all-reduce.9.cloned.1.call-done = (f32[2,128,256]{2,1,0:T(8,128)}, f32[2,256,128]{2,1,0:T(8,128)}) async-done(((f32[2,128,256]{2,1,0:T(8,128)}, f32[2,256,128]{2,1,0:T(8,128)}), (f32[2,128,256]{2,1,0:T(8,128)}, f32[2,256,128]{2,1,0:T(8,128)})) %all-reduce.9.cloned.1.call-update) | async-done | bytes 524304 | tf_op jit(solution)/shard_map/psum | solution.py:16
  144.5 1.7 %copy.16 = f32[2,128,256]{2,1,0:T(8,128)} copy(f32[2,128,256]{2,1,0:T(8,128)} %get-tuple-element.75) | data formatting | bytes 524288
  146.2 0.7 copy.17
  (101 shorter events, 0.3 us)
Async XLA Ops:
  7.2 2.1 %copy-start = (f32[1,1024,128]{2,1,0:T(8,128)S(1)}, f32[1,1024,128]{2,1,0:T(8,128)}, u32[]{:S(2)}) copy-start(f32[1,1024,128]{2,1,0:T(8,128)} %param.6) | copy-start | bytes 1572868
  7.2 95.6 %all-reduce.7.cloned.1.call-start = ((), (), s32[]{:S(2)}) async-start(), calls=%async_computation | async-start | bytes 1048576 | tf_op jit(solution)/shard_map/psum | solution.py:16
  8.0 1.3 copy-start.16
  8.0 11.6 %copy-start.18 = (f32[128]{0:T(128)}, f32[128]{0:T(128)S(1)}, u32[]{:S(2)}) copy-start(f32[128]{0:T(128)S(1)} %get-tuple-element.66) | copy-start | bytes 1540
  9.5 6.0 %copy-start.20 = (f32[2,7,128]{2,0,1:T(2,128)S(1)}, f32[2,7,128]{2,0,1:T(2,128)}, u32[]{:S(2)}) copy-start(f32[2,7,128]{2,0,1:T(2,128)} %param.9) | copy-start | bytes 21508
  9.5 6.1 %collective-permute-start.1 = (f32[1,48,128]{2,1,0:T(8,128)S(1)}, f32[1,48,128]{2,1,0:T(8,128)S(1)}, u32[]{:S(2)}, u32[]{:S(2)}) collective-permute-start(f32[1,48,128]{2,1,0:T(8,128)S(1)} %get-tuple-element.50), channel_id=1, source_target_pairs={{4,0},{8,4},{12,8},{5,1},{9,5},{13,9},{6,2},{10,6},{14,10},{7,3},{... | collective-permute-start | bytes 73736 | tf_op jit(solution)/shard_map/ppermute | solution.py:31
  10.8 5.6 %collective-permute-start = (f32[1,48,128]{2,1,0:T(8,128)S(1)}, f32[1,48,128]{2,1,0:T(8,128)S(1)}, u32[]{:S(2)}, u32[]{:S(2)}) collective-permute-start(f32[1,48,128]{2,1,0:T(8,128)S(1)} %get-tuple-element.51), channel_id=1, source_target_pairs={{0,4},{4,8},{8,12},{1,5},{5,9},{9,13},{2,6},{6,10},{10,14},{3,7},{... | collective-permute-start | bytes 73736 | tf_op jit(solution)/shard_map/ppermute | solution.py:28
  15.5 0.9 copy-start.21
  15.5 0.9 copy-start.23
  15.5 0.9 copy-start.25
  15.5 0.9 copy-start.27
  15.5 0.9 copy-start.29
  15.6 0.9 copy-start.31
  15.6 0.9 copy-start.33
  15.6 16.4 %copy-start.35 = (f32[128]{0:T(128)}, f32[128]{0:T(128)S(1)}, u32[]{:S(2)}) copy-start(f32[128]{0:T(128)S(1)} %get-tuple-element.52) | copy-start | bytes 1540
  15.6 16.4 %copy-start.37 = (f32[128]{0:T(128)}, f32[128]{0:T(128)S(1)}, u32[]{:S(2)}) copy-start(f32[128]{0:T(128)S(1)} %get-tuple-element.53) | copy-start | bytes 1540
  15.6 16.4 %copy-start.39 = (f32[128]{0:T(128)}, f32[128]{0:T(128)S(1)}, u32[]{:S(2)}) copy-start(f32[128]{0:T(128)S(1)} %get-tuple-element.54) | copy-start | bytes 1540
  15.6 16.4 %copy-start.41 = (f32[128]{0:T(128)}, f32[128]{0:T(128)S(1)}, u32[]{:S(2)}) copy-start(f32[128]{0:T(128)S(1)} %get-tuple-element.55) | copy-start | bytes 1540
  15.6 16.4 %copy-start.43 = (f32[128]{0:T(128)}, f32[128]{0:T(128)S(1)}, u32[]{:S(2)}) copy-start(f32[128]{0:T(128)S(1)} %get-tuple-element.62) | copy-start | bytes 1540
  15.6 16.4 %copy-start.45 = (f32[128]{0:T(128)}, f32[128]{0:T(128)S(1)}, u32[]{:S(2)}) copy-start(f32[128]{0:T(128)S(1)} %get-tuple-element.64) | copy-start | bytes 1540
  15.6 16.4 %copy-start.47 = (f32[128]{0:T(128)}, f32[128]{0:T(128)S(1)}, u32[]{:S(2)}) copy-start(f32[128]{0:T(128)S(1)} %get-tuple-element.65) | copy-start | bytes 1540
  15.7 1.1 copy-start.11
  16.4 0.6 copy-start.13
  16.5 1.0 copy-start.9
  17.4 1.0 copy-start.49
  18.4 1.2 copy-start.1
  19.9 11.2 %collective-permute-start.3 = (f32[1,768,128]{2,1,0:T(8,128)S(1)}, f32[1,768,128]{2,1,0:T(8,128)S(1)}, u32[]{:S(2)}, u32[]{:S(2)}) collective-permute-start(f32[1,768,128]{2,1,0:T(8,128)S(1)} %get-tuple-element.48), channel_id=1, source_target_pairs={{4,0},{8,4},{12,8},{5,1},{9,5},{13,9},{6,2},{10,6},{14,10},{7,3},{... | collective-permute-start | bytes 1179656 | tf_op jit(solution)/shard_map/ppermute | solution.py:31
  21.2 10.8 %collective-permute-start.2 = (f32[1,768,128]{2,1,0:T(8,128)S(1)}, f32[1,768,128]{2,1,0:T(8,128)S(1)}, u32[]{:S(2)}, u32[]{:S(2)}) collective-permute-start(f32[1,768,128]{2,1,0:T(8,128)S(1)} %get-tuple-element.49), channel_id=1, source_target_pairs={{0,4},{4,8},{8,12},{1,5},{5,9},{9,13},{2,6},{6,10},{10,14},{3,7},{... | collective-permute-start | bytes 1179656 | tf_op jit(solution)/shard_map/ppermute | solution.py:28
  32.3 2.0 %copy-start.6 = (f32[1,1024,128]{2,1,0:T(8,128)S(1)}, f32[1,1024,128]{2,1,0:T(8,128)}, u32[]{:S(2)}) copy-start(f32[1,1024,128]{2,1,0:T(8,128)} %param.7) | copy-start | bytes 1572868
  33.3 1.0 copy-start.3
  35.4 1.7 %copy-start.5 = (f32[1024,256]{1,0:T(8,128)}, f32[1024,256]{1,0:T(8,128)S(1)}, u32[]{:S(2)}) copy-start(f32[1024,256]{1,0:T(8,128)S(1)} %convolution_multiply_fusion.1) | copy-start | bytes 3145732
  38.1 11.3 %collective-permute-start.4 = (f32[1,768,128]{2,1,0:T(8,128)}, f32[1,768,128]{2,1,0:T(8,128)S(1)}, u32[]{:S(2)}, u32[]{:S(2)}) collective-permute-start(f32[1,768,128]{2,1,0:T(8,128)} %get-tuple-element.46), channel_id=1, source_target_pairs={{0,4},{4,8},{8,12},{1,5},{5,9},{9,13},{2,6},{6,10},{10,14},{3,7},{... | collective-permute-start | bytes 1179656 | tf_op jit(solution)/shard_map/ppermute | solution.py:28
  42.2 9.8 %collective-permute-start.5 = (f32[1,768,128]{2,1,0:T(8,128)}, f32[1,768,128]{2,1,0:T(8,128)}, u32[]{:S(2)}, u32[]{:S(2)}) collective-permute-start(f32[1,768,128]{2,1,0:T(8,128)} %get-tuple-element.47), channel_id=1, source_target_pairs={{4,0},{8,4},{12,8},{5,1},{9,5},{13,9},{6,2},{10,6},{14,10},{7,3},{... | collective-permute-start | bytes 1179656 | tf_op jit(solution)/shard_map/ppermute | solution.py:31
  45.0 2.4 %copy-start.4 = (f32[1024,256]{1,0:T(8,128)S(1)}, f32[1024,256]{1,0:T(8,128)}, u32[]{:S(2)}) copy-start(f32[1024,256]{1,0:T(8,128)} %copy-done.3) | copy-start | bytes 3145732
  45.0 2.4 %copy-start.7 = (f32[1,1024,128]{2,1,0:T(8,128)S(1)}, f32[1,1024,128]{2,1,0:T(8,128)}, u32[]{:S(2)}) copy-start(f32[1,1024,128]{2,1,0:T(8,128)} %param.7) | copy-start | bytes 1572868
  47.4 4.6 %copy-start.19 = (f32[128]{0:T(128)S(1)}, f32[128]{0:T(128)}, u32[]{:S(2)}) copy-start(f32[128]{0:T(128)} %copy-done.18) | copy-start | bytes 1540
  47.4 4.6 %copy-start.36 = (f32[128]{0:T(128)S(1)}, f32[128]{0:T(128)}, u32[]{:S(2)}) copy-start(f32[128]{0:T(128)} %copy-done.35) | copy-start | bytes 1540
  47.4 4.6 %copy-start.38 = (f32[128]{0:T(128)S(1)}, f32[128]{0:T(128)}, u32[]{:S(2)}) copy-start(f32[128]{0:T(128)} %copy-done.37) | copy-start | bytes 1540
  47.4 4.6 %copy-start.40 = (f32[128]{0:T(128)S(1)}, f32[128]{0:T(128)}, u32[]{:S(2)}) copy-start(f32[128]{0:T(128)} %copy-done.39) | copy-start | bytes 1540
  47.4 4.6 %copy-start.42 = (f32[128]{0:T(128)S(1)}, f32[128]{0:T(128)}, u32[]{:S(2)}) copy-start(f32[128]{0:T(128)} %copy-done.41) | copy-start | bytes 1540
  47.4 4.6 %copy-start.44 = (f32[128]{0:T(128)S(1)}, f32[128]{0:T(128)}, u32[]{:S(2)}) copy-start(f32[128]{0:T(128)} %copy-done.43) | copy-start | bytes 1540
  47.4 4.6 %copy-start.46 = (f32[128]{0:T(128)S(1)}, f32[128]{0:T(128)}, u32[]{:S(2)}) copy-start(f32[128]{0:T(128)} %copy-done.45) | copy-start | bytes 1540
  47.4 4.6 %copy-start.48 = (f32[128]{0:T(128)S(1)}, f32[128]{0:T(128)}, u32[]{:S(2)}) copy-start(f32[128]{0:T(128)} %copy-done.47) | copy-start | bytes 1540
  53.7 1.2 copy-start.2
  54.9 1.9 %copy-start.50 = (f32[2,256,128]{2,1,0:T(8,128)S(1)}, f32[2,256,128]{2,1,0:T(8,128)}, u32[]{:S(2)}) copy-start(f32[2,256,128]{2,1,0:T(8,128)} %param.11) | copy-start | bytes 786436
  58.0 1.1 copy-start.10
  58.0 1.1 copy-start.12
  58.0 1.1 copy-start.14
  60.1 6.4 %collective-permute-start.6 = (f32[1,48,128]{2,1,0:T(8,128)S(1)}, f32[1,48,128]{2,1,0:T(8,128)S(1)}, u32[]{:S(2)}, u32[]{:S(2)}) collective-permute-start(f32[1,48,128]{2,1,0:T(8,128)S(1)} %get-tuple-element.44), channel_id=1, source_target_pairs={{0,4},{4,8},{8,12},{1,5},{5,9},{9,13},{2,6},{6,10},{10,14},{3,7},{... | collective-permute-start | bytes 73736 | tf_op jit(solution)/shard_map/ppermute | solution.py:28
  62.9 4.6 %collective-permute-start.7 = (f32[1,48,128]{2,1,0:T(8,128)S(1)}, f32[1,48,128]{2,1,0:T(8,128)S(1)}, u32[]{:S(2)}, u32[]{:S(2)}) collective-permute-start(f32[1,48,128]{2,1,0:T(8,128)S(1)} %get-tuple-element.45), channel_id=1, source_target_pairs={{4,0},{8,4},{12,8},{5,1},{9,5},{13,9},{6,2},{10,6},{14,10},{7,3},{... | collective-permute-start | bytes 73736 | tf_op jit(solution)/shard_map/ppermute | solution.py:31
  65.7 78.8 %all-reduce.9.cloned.1.call-start = ((), (), s32[]{:S(2)}) async-start(), calls=%async_computation.1 | async-start | bytes 1048576 | tf_op jit(solution)/shard_map/psum | solution.py:16
  65.8 0.7 copy-start.15
  66.5 1.1 copy-start.17
  66.5 1.1 copy-start.22
  66.5 1.1 copy-start.24
  66.5 1.1 copy-start.26
  66.5 1.1 copy-start.28
  66.5 1.1 copy-start.30
  66.5 1.1 copy-start.32
  66.5 1.1 copy-start.34
  144.5 1.7 %copy-start.8 = (f32[2,256,128]{2,1,0:T(8,128)S(1)}, f32[2,256,128]{2,1,0:T(8,128)}, u32[]{:S(2)}) copy-start(f32[2,256,128]{2,1,0:T(8,128)} %get-tuple-element.76) | copy-start | bytes 786436
Sparse Core Ops, SparseCore 0:
  65.8 36.9 all-reduce.6
  105.2 39.2 all-reduce.8
